TPU v7x, 256 devices: a whole 4x4x8 slice. The times are simulated.
256 devices in a mesh: leaf: 16 (over z, core), group: 16 (over x, y).
Axes of the slice: x: 4, y: 4, z: 8, core: 2. Of those that a mesh axis runs over, the one named last changes fastest.
Arguments:
- tile_fields: bfloat16 [2048, 32, 32, 512], P(('leaf', 'group')), may hold values from -2500 to 2500
- routes: int32 [256, 8], P(('leaf', 'group')), may hold values from 0 to 15, as said below
- counts: int32 [256], P(('leaf', 'group')), may hold values from 5 to 8
Outputs:
- factor: float32 [16, 16], replicated
- mode_blocks: float32 [4096, 256, 256], P(('leaf', 'group'))
Inputs may be any that keep to these rules, and one draw needn't show every extreme that they name: `routes`: the 8 entries of a device are distinct. In every group some leaf index is named by an occupied slot of every device of the group, and every leaf index is named by an occupied slot of some device of the group.
All inputs are finite; a program needn't handle non-finite values.
Results may differ from a plain program's by a relative error of at most 0.012.
The roundings to bfloat16 on the way count: a program that leaves them out, or rounds other values in their place, can miss the bound.
Values may be sent and summed in bfloat16 or wider, within the bound.
A program may use at most 128 MiB of HBM per device.

v0:
```python
import jax
import jax.numpy as jnp
from jax import lax
from jax.sharding import PartitionSpec as P


def smoother(length):
    half_edge = length // 2
    row_index = jnp.arange(half_edge)[:, None]
    col_index = jnp.arange(length)[None, :]
    offset = (col_index - 2 * row_index).astype(jnp.float32)
    tap_offsets = jnp.arange(-4, 5).astype(jnp.float32)
    normalizer = jnp.sum(jnp.exp(-tap_offsets * tap_offsets / 4.5))
    weights = jnp.where(jnp.abs(offset) <= 4.0, jnp.exp(-offset * offset / 4.5) / normalizer, 0.0)
    return weights.astype(jnp.bfloat16)


def cholesky_upper(gram):
    order = gram.shape[0]
    positions = jnp.arange(order)
    upper = jnp.zeros_like(gram)
    for row_index in range(order):
        partial_row = gram[row_index] - jnp.sum(upper[:, row_index][:, None] * upper, axis=0)
        pivot = jnp.sqrt(partial_row[row_index])
        new_row = jnp.where(
            positions >= row_index, partial_row / pivot, jnp.zeros_like(partial_row)
        )
        upper = upper.at[row_index].set(new_row)
    return upper


def invert_upper(upper):
    order = upper.shape[0]
    positions = jnp.arange(order)
    identity = jnp.eye(order, dtype=upper.dtype)
    result = jnp.zeros_like(upper)
    for row_index in range(order - 1, -1, -1):
        off_diagonal = jnp.where(
            positions > row_index, upper[row_index], jnp.zeros_like(upper[row_index])
        )
        partial_row = identity[row_index] - jnp.sum(off_diagonal[:, None] * result, axis=0)
        result = result.at[row_index].set(partial_row / upper[row_index, row_index])
    return result


def filter_tiles(payload):
    slots_here = payload.shape[0]
    tile_edge = payload.shape[1]
    half_edge = tile_edge // 2
    snapshots = payload.shape[3] // tile_edge
    weights = smoother(tile_edge)
    first_pass = jnp.einsum(
        "ix,sxr->sir",
        weights,
        payload.reshape(slots_here, tile_edge, tile_edge * tile_edge * snapshots),
        preferred_element_type=jnp.float32,
    ).astype(jnp.bfloat16)
    second_pass = jnp.einsum(
        "jy,siyc->sijc",
        weights,
        first_pass.reshape(slots_here, half_edge, tile_edge, tile_edge * snapshots),
        preferred_element_type=jnp.float32,
    ).astype(jnp.bfloat16)
    depth_table = jnp.kron(weights, jnp.eye(snapshots, dtype=jnp.bfloat16))
    flat_second = second_pass.reshape(slots_here * half_edge * half_edge, tile_edge * snapshots)
    third_pass = lax.dot_general(
        flat_second, depth_table, (((1,), (1,)), ((), ())), preferred_element_type=jnp.float32
    ).astype(jnp.bfloat16)
    return third_pass.reshape(slots_here, half_edge * half_edge, half_edge * snapshots)


def gram_matrix(filtered, snapshots):
    flat_rows = filtered.reshape(-1, filtered.shape[-1] // snapshots, snapshots)
    return lax.dot_general(
        flat_rows, flat_rows, (((0, 1), (0, 1)), ((), ())), preferred_element_type=jnp.float32
    )


def place_tiles(payload, route_row, count_here, leaves):
    buffer = jnp.zeros((leaves,) + payload.shape[1:], payload.dtype)
    for slot_index in range(payload.shape[0]):
        tile_piece = jnp.where(
            slot_index < count_here, payload[slot_index], jnp.zeros_like(payload[slot_index])
        )
        buffer = lax.dynamic_update_slice_in_dim(buffer, tile_piece[None], route_row[slot_index], 0)
    return buffer


def shards(tile_fields, routes, counts):
    leaves = lax.axis_size("leaf")
    groups = lax.axis_size("group")
    slots_here = tile_fields.shape[0]
    tile_edge = tile_fields.shape[1]
    snapshots = tile_fields.shape[3] // tile_edge
    half_edge = tile_edge // 2
    rows_all = half_edge**3 * slots_here * leaves * groups
    route_row = routes[0]
    count_here = counts[0]
    incoming = lax.all_to_all(
        place_tiles(tile_fields, route_row, count_here, leaves),
        "leaf",
        split_axis=0,
        concat_axis=0,
        tiled=True,
    )
    arrived = filter_tiles(incoming)
    local_gram = gram_matrix(arrived, snapshots)
    summed = lax.psum(local_gram, ("leaf", "group"))
    factor = cholesky_upper(summed / rows_all)
    inverse = invert_upper(factor)
    block_inverse = jnp.kron(jnp.eye(half_edge, dtype=jnp.float32), inverse)
    flat_rows = arrived.reshape(leaves * half_edge * half_edge, half_edge * snapshots).astype(
        jnp.float32
    )
    mode_blocks = jnp.dot(flat_rows, block_inverse, precision=lax.Precision.HIGHEST)
    return (factor, mode_blocks.reshape(leaves, half_edge * half_edge, half_edge * snapshots))


def solution(mesh):
    return jax.shard_map(
        shards,
        mesh=mesh,
        in_specs=(
            P(("leaf", "group"), None, None, None),
            P(("leaf", "group"), None),
            P(("leaf", "group")),
        ),
        out_specs=(P(), P(("leaf", "group"), None, None)),
        check_vma=False,
    )
```

profile of v0, /device:TPU:1, one launch (start us, length us, event | category | flops | bytes accessed | tf_op | source)
XLA Modules:
  0.0 622.5 jit_solution(9531453409262674630)
XLA Ops:
  0.6 1.6 fusion.44
  18.1 8.0 %broadcast_in_dim.9 = bf16[16,32,32,512]{3,2,1,0:T(8,128)(2,1)} broadcast(bf16[]{:T(256)} %constant.803.clone.1), dimensions={} | broadcast | bytes 16777218 | tf_op jit(solution)/shard_map/broadcast_in_dim | solution.py:80
  26.4 1.2 select_dynamic-update-slice_fusion.7
  27.7 1.2 select_dynamic-update-slice_fusion.6
  28.9 1.2 select_dynamic-update-slice_fusion.5
  30.1 1.2 select_dynamic-update-slice_fusion.4
  31.3 1.2 select_dynamic-update-slice_fusion.3
  32.5 1.3 select_dynamic-update-slice_fusion.2
  33.8 1.2 select_dynamic-update-slice_fusion.1
  35.0 1.2 select_dynamic-update-slice_fusion
  36.2 10.0 %all-to-all-start = ((bf16[16,32,32,512]{3,2,1,0:T(8,128)(2,1)}), bf16[16,32,32,512]{3,2,1,0:T(8,128)(2,1)}, u32[]{:S(2)}, u32[]{:S(2)}) async-start(bf16[16,32,32,512]{3,2,1,0:T(8,128)(2,1)} %select_dynamic-update-slice_fusion), calls=%async_computation | async-start | bytes 33554432 | tf_op jit(solution)/shard_map/all_to_all | solution.py:99
  46.8 0.7 fusion.11
  47.8 3.6 mul.363
  51.4 357.9 %all-to-all-done = bf16[16,32,32,512]{3,2,1,0:T(8,128)(2,1)} async-done(((bf16[16,32,32,512]{3,2,1,0:T(8,128)(2,1)}), bf16[16,32,32,512]{3,2,1,0:T(8,128)(2,1)}, u32[]{:S(2)}, u32[]{:S(2)}) %all-to-all-start) | async-done | bytes 16777248 | tf_op jit(solution)/shard_map/all_to_all | solution.py:99
  409.3 25.6 %reshape.1109 = bf16[16,32,16384]{2,1,0:T(8,128)(2,1)} reshape(bf16[16,32,32,512]{3,2,1,0:T(8,128)(2,1)} %all-to-all-done) | data formatting | bytes 33554432 | tf_op jit(solution)/shard_map/reshape | solution.py:55
  434.9 12.1 %convolution_convert_fusion = bf16[16,16384,16]{1,2,0:T(8,128)(2,1)} fusion(bf16[16,32,16384]{2,1,0:T(8,128)(2,1)} %reshape.1109, f32[]{:T(128)} %fusion.18, s32[16]{0:T(128)S(1)} %iota_multiply_fusion), kind=kOutput, calls=%fused_computation | convolution fusion | flops 272634880 | bytes 25165892 | tf_op jit(solution)/shard_map/ix,sxr->sir/dot_general | solution.py:52
  446.9 10.4 %copy.9 = bf16[32,8,32,512]{3,2,1,0:T(8,128)(2,1)} copy(bf16[32,8,32,512]{3,1,2,0:T(8,128)(2,1)} %bitcast.268) | data formatting | bytes 16777216
  457.3 5.3 fusion.2
  462.6 2.6 convolution_convert_fusion.1
  465.3 2.9 copy.7
  468.2 1.0 convolution_bitcast_fusion
  469.2 78.0 %psum.7 = f32[16,16]{1,0:T(8,128)S(1)} all-reduce(f32[16,16]{1,0:T(8,128)S(1)} %convolution_bitcast_fusion), channel_id=1, replica_groups=mesh['leaf'=16,'group'=16] {'leaf','group'}, use_global_device_ids=true, to_apply=%region_1.2 | all-reduce | flops 256 | bytes 2048 | tf_op jit(solution)/shard_map/psum | solution.py:108
  552.2 0.7 compare_select_fusion.30
  553.2 0.7 bitcast_subtract_fusion.24
  555.2 0.7 compare_select_fusion.29
  556.2 0.7 bitcast_subtract_fusion.22
  558.1 0.7 compare_select_fusion.28
  559.1 0.7 bitcast_subtract_fusion.20
  562.1 0.7 bitcast_subtract_fusion.18
  564.0 0.7 compare_select_fusion.26
  565.0 0.7 bitcast_subtract_fusion.16
  569.9 0.7 compare_select_fusion.24
  570.9 0.7 bitcast_subtract_fusion.12
  572.9 0.7 compare_select_fusion.23
  573.9 0.7 bitcast_subtract_fusion.10
  575.8 0.7 compare_select_fusion.22
  576.8 0.7 bitcast_subtract_fusion.8
  578.8 0.7 compare_select_fusion.21
  579.8 0.7 bitcast_subtract_fusion.6
  581.7 0.7 compare_select_fusion.20
  582.7 0.7 bitcast_subtract_fusion.4
  584.7 0.7 compare_select_fusion.19
  585.7 0.7 bitcast_subtract_fusion.2
  587.6 0.7 compare_select_fusion.18
  588.6 0.7 bitcast_subtract_fusion
  592.6 0.7 fusion.43
  593.3 1.2 fusion.35
  595.3 1.3 fusion.33
  596.7 1.3 fusion.32
  598.1 1.2 fusion.31
  599.5 1.4 fusion.30
  601.0 1.4 fusion.29
  602.5 1.3 fusion.28
  603.9 1.3 fusion.27
  605.3 1.4 fusion.26
  606.8 1.4 fusion.25
  608.3 1.3 fusion.24
  609.7 1.3 fusion.23
  611.1 1.3 fusion.22
  612.6 1.2 fusion.21
  613.9 1.3 fusion.20
  615.2 0.9 broadcast_multiply_fusion
  616.2 0.9 reshape.1115
  617.1 5.4 fusion.45
  (117 shorter events, 22.2 us)
Async XLA Ops:
  18.1 8.4 %copy-start = (bf16[8,32,32,512]{3,2,1,0:T(8,128)(2,1)S(1)}, bf16[8,32,32,512]{3,2,1,0:T(8,128)(2,1)}, u32[]{:S(2)}) copy-start(bf16[8,32,32,512]{3,2,1,0:T(8,128)(2,1)} %param.67) | copy-start | bytes 25165828
  36.2 373.1 %all-to-all-start = ((bf16[16,32,32,512]{3,2,1,0:T(8,128)(2,1)}), bf16[16,32,32,512]{3,2,1,0:T(8,128)(2,1)}, u32[]{:S(2)}, u32[]{:S(2)}) async-start(bf16[16,32,32,512]{3,2,1,0:T(8,128)(2,1)} %select_dynamic-update-slice_fusion), calls=%async_computation | async-start | bytes 33554432 | tf_op jit(solution)/shard_map/all_to_all | solution.py:99
  51.4 543.2 %copy-start.2 = (f32[16,16]{1,0:T(8,128)}, f32[16,16]{1,0:T(8,128)S(1)}, u32[]{:S(2)}) copy-start(f32[16,16]{1,0:T(8,128)S(1)} %fusion.9) | copy-start | bytes 3076
  547.2 3.1 copy-start.3
  592.5 30.0 %copy-start.1 = (f32[16,16]{1,0:T(8,128)}, f32[16,16]{1,0:T(8,128)S(1)}, u32[]{:S(2)}) copy-start(f32[16,16]{1,0:T(8,128)S(1)} %scatter.131) | copy-start | bytes 3076
where the time goes:
time: 626 us; the launch traced here: 623 us
  waiting for transfers between devices  358 us (57%)
  blocking collectives  78 us (12%)
  local copies, waits for them, and re-layouts  67.7 us (11%)
  other arithmetic  55.3 us (9%)
  between operations  27.2 us (4%)
  matrix products  26.4 us (4%)
  starting transfers between devices  9.99 us (2%)
    all_to_all x1, waiting for transfers between devices, shards(): lax.all_to_all(place_tiles(tile_fields, route_row, count_here, leaves), '...  358 us
    psum x1, blocking collectives, shards(): summed = lax.psum(local_gram, ('leaf', 'group'))  78 us
    reshape x1, local copies, waits for them, and re-layouts, filter_tiles(): payload.reshape(slots_here, tile_edge, tile_edge * tile_edge * snapshots)  25.6 us
    div x16, other arithmetic, invert_upper(): result = result.at[row_index].set(partial_row / upper[row_index, row_index])  20.2 us
  transfers between devices with their start and end apart: 1, of which 1 were waited for; matrix products, arithmetic and copies ran while one was open for 1% of the time, Pallas kernels for 0%

commit v1 on v0

--- a/solution.py
+++ b/solution.py
@@ -105,7 +105,7 @@
     )
     arrived = filter_tiles(incoming)
     local_gram = gram_matrix(arrived, snapshots)
-    summed = lax.psum(local_gram, ("leaf", "group"))
+    summed = jnp.sum(lax.all_gather(local_gram, ("leaf", "group")), axis=0)
     factor = cholesky_upper(summed / rows_all)
     inverse = invert_upper(factor)
     block_inverse = jnp.kron(jnp.eye(half_edge, dtype=jnp.float32), inverse)

time: 626 us -> 682 us (1.089)
  blocking collectives: 78 us -> 129 us
    all_gather x0 -> x1, blocking collectives: none -> 129 us  [shards(): summed = jnp.sum(lax.all_gather(local_gram, ('leaf', 'group')), axis=0)]
    psum x1 -> x0, blocking collectives: 78 us -> none  [shards(): summed = lax.psum(local_gram, ('leaf', 'group'))]
where the time goes in v1:
time: 682 us; the launch traced here: 679 us
  waiting for transfers between devices  358 us (52%)
  blocking collectives  129 us (19%)
  local copies, waits for them, and re-layouts  70.2 us (10%)
  other arithmetic  58.5 us (9%)
  between operations  28.3 us (4%)
  matrix products  24.8 us (4%)
  starting transfers between devices  9.99 us (1%)
    all_to_all x1, waiting for transfers between devices, shards(): lax.all_to_all(place_tiles(tile_fields, route_row, count_here, leaves), '...  358 us
    all_gather x1, blocking collectives, shards(): summed = jnp.sum(lax.all_gather(local_gram, ('leaf', 'group')), axis=0)  129 us
    reshape x1, local copies, waits for them, and re-layouts, filter_tiles(): payload.reshape(slots_here, tile_edge, tile_edge * tile_edge * snapshots)  25.6 us
    div x16, other arithmetic, invert_upper(): result = result.at[row_index].set(partial_row / upper[row_index, row_index])  20.1 us
  transfers between devices with their start and end apart: 1, of which 1 were waited for; matrix products, arithmetic and copies ran while one was open for 1% of the time, Pallas kernels for 0%

profile of v1, /device:TPU:1, one launch (start us, length us, event | category | flops | bytes accessed | tf_op | source)
XLA Modules:
  0.0 678.5 jit_solution(9352670388414848968)
XLA Ops:
  0.6 1.6 fusion.44
  18.1 8.0 %broadcast_in_dim.9 = bf16[16,32,32,512]{3,2,1,0:T(8,128)(2,1)} broadcast(bf16[]{:T(256)} %constant.803.clone.1), dimensions={} | broadcast | bytes 16777218 | tf_op jit(solution)/shard_map/broadcast_in_dim | solution.py:80
  26.4 1.2 select_dynamic-update-slice_fusion.7
  27.7 1.2 select_dynamic-update-slice_fusion.6
  28.9 1.2 select_dynamic-update-slice_fusion.5
  30.1 1.2 select_dynamic-update-slice_fusion.4
  31.3 1.2 select_dynamic-update-slice_fusion.3
  32.5 1.3 select_dynamic-update-slice_fusion.2
  33.8 1.2 select_dynamic-update-slice_fusion.1
  35.0 1.2 select_dynamic-update-slice_fusion
  36.2 10.0 %all-to-all-start = ((bf16[16,32,32,512]{3,2,1,0:T(8,128)(2,1)}), bf16[16,32,32,512]{3,2,1,0:T(8,128)(2,1)}, u32[]{:S(2)}, u32[]{:S(2)}) async-start(bf16[16,32,32,512]{3,2,1,0:T(8,128)(2,1)} %select_dynamic-update-slice_fusion), calls=%async_computation | async-start | bytes 33554432 | tf_op jit(solution)/shard_map/all_to_all | solution.py:99
  46.8 0.7 fusion.11
  47.8 3.6 mul.363
  51.4 357.9 %all-to-all-done = bf16[16,32,32,512]{3,2,1,0:T(8,128)(2,1)} async-done(((bf16[16,32,32,512]{3,2,1,0:T(8,128)(2,1)}), bf16[16,32,32,512]{3,2,1,0:T(8,128)(2,1)}, u32[]{:S(2)}, u32[]{:S(2)}) %all-to-all-start) | async-done | bytes 16777248 | tf_op jit(solution)/shard_map/all_to_all | solution.py:99
  409.3 25.6 %reshape.1109 = bf16[16,32,16384]{2,1,0:T(8,128)(2,1)} reshape(bf16[16,32,32,512]{3,2,1,0:T(8,128)(2,1)} %all-to-all-done) | data formatting | bytes 33554432 | tf_op jit(solution)/shard_map/reshape | solution.py:55
  434.9 12.1 %convolution_convert_fusion = bf16[16,16384,16]{1,2,0:T(8,128)(2,1)} fusion(bf16[16,32,16384]{2,1,0:T(8,128)(2,1)} %reshape.1109, f32[]{:T(128)} %fusion.18, s32[16]{0:T(128)S(1)} %iota_multiply_fusion), kind=kOutput, calls=%fused_computation | convolution fusion | flops 272634880 | bytes 25165892 | tf_op jit(solution)/shard_map/ix,sxr->sir/dot_general | solution.py:52
  446.9 10.4 %copy.9 = bf16[32,8,32,512]{3,2,1,0:T(8,128)(2,1)} copy(bf16[32,8,32,512]{3,1,2,0:T(8,128)(2,1)} %bitcast.269) | data formatting | bytes 16777216
  457.3 5.3 fusion.2
  462.6 2.6 convolution_convert_fusion.1
  465.3 2.9 copy.7
  468.2 1.0 convolution_bitcast_fusion
  469.1 128.9 %all-gather = f32[4096,16]{1,0:T(8,128)} all-gather(f32[16,16]{1,0:T(8,128)S(1)} %convolution_bitcast_fusion), channel_id=2, replica_groups=mesh['leaf'=16,'group'=16] {'leaf','group'}, dimensions={0}, use_global_device_ids=true | all-gather | bytes 263168 | tf_op jit(solution)/shard_map/all_gather | solution.py:108
  598.0 1.9 reduce_sum.368
  605.4 0.7 compare_select_fusion.30
  606.4 0.7 bitcast_subtract_fusion.24
  609.5 0.7 bitcast_subtract_fusion.22
  611.6 0.7 compare_select_fusion.28
  612.6 0.7 bitcast_subtract_fusion.20
  615.7 0.7 bitcast_subtract_fusion.18
  618.8 0.7 bitcast_subtract_fusion.16
  621.8 0.7 bitcast_subtract_fusion.14
  623.9 0.7 compare_select_fusion.24
  624.9 0.7 bitcast_subtract_fusion.12
  627.0 0.7 compare_select_fusion.23
  628.0 0.7 bitcast_subtract_fusion.10
  630.1 0.7 compare_select_fusion.22
  631.1 0.7 bitcast_subtract_fusion.8
  633.2 0.7 compare_select_fusion.21
  634.2 0.7 bitcast_subtract_fusion.6
  636.3 0.7 compare_select_fusion.20
  637.3 0.7 bitcast_subtract_fusion.4
  639.4 0.7 compare_select_fusion.19
  640.4 0.7 bitcast_subtract_fusion.2
  642.5 0.7 compare_select_fusion.18
  643.5 0.7 bitcast_subtract_fusion
  647.4 0.7 fusion.43
  648.1 1.3 fusion.35
  650.2 1.3 fusion.33
  651.6 1.2 fusion.32
  653.0 1.3 fusion.31
  654.4 1.3 fusion.30
  655.9 1.3 fusion.29
  657.3 1.3 fusion.28
  658.7 1.4 fusion.27
  660.2 1.2 fusion.26
  661.5 1.4 fusion.25
  663.0 1.2 fusion.24
  664.4 1.3 fusion.23
  665.8 1.3 fusion.22
  667.2 1.3 fusion.21
  668.6 1.3 fusion.20
  670.0 2.3 broadcast_multiply_fusion
  672.2 2.4 reshape.1116
  674.7 3.8 fusion.45
  (120 shorter events, 24.0 us)
Async XLA Ops:
  18.1 8.4 %copy-start.1 = (bf16[8,32,32,512]{3,2,1,0:T(8,128)(2,1)S(1)}, bf16[8,32,32,512]{3,2,1,0:T(8,128)(2,1)}, u32[]{:S(2)}) copy-start(bf16[8,32,32,512]{3,2,1,0:T(8,128)(2,1)} %param.67) | copy-start | bytes 25165828
  36.2 373.1 %all-to-all-start = ((bf16[16,32,32,512]{3,2,1,0:T(8,128)(2,1)}), bf16[16,32,32,512]{3,2,1,0:T(8,128)(2,1)}, u32[]{:S(2)}, u32[]{:S(2)}) async-start(bf16[16,32,32,512]{3,2,1,0:T(8,128)(2,1)} %select_dynamic-update-slice_fusion), calls=%async_computation | async-start | bytes 33554432 | tf_op jit(solution)/shard_map/all_to_all | solution.py:99
  51.4 598.1 %copy-start.3 = (f32[16,16]{1,0:T(8,128)}, f32[16,16]{1,0:T(8,128)S(1)}, u32[]{:S(2)}) copy-start(f32[16,16]{1,0:T(8,128)S(1)} %fusion.9) | copy-start | bytes 3076
  469.1 205.5 %copy-start = (bf16[4096,256]{1,0:T(8,128)(2,1)S(1)}, bf16[4096,256]{1,0:T(8,128)(2,1)}, u32[]{:S(2)}) copy-start(bf16[4096,256]{1,0:T(8,128)(2,1)} %convolution_convert_fusion.1) | copy-start | bytes 6291460
  599.9 3.4 copy-start.4
  647.4 31.2 %copy-start.2 = (f32[16,16]{1,0:T(8,128)}, f32[16,16]{1,0:T(8,128)S(1)}, u32[]{:S(2)}) copy-start(f32[16,16]{1,0:T(8,128)S(1)} %scatter.131) | copy-start | bytes 3076
